TPU v7x, 256 devices: a whole 4x4x8 slice. The times are simulated.
256 devices in a mesh: tm: 32 (over z, y), table: 8 (over x, core).
Axes of the slice: x: 4, y: 4, z: 8, core: 2. Of those that a mesh axis runs over, the one named last changes fastest.
Arguments:
- out_grad: bfloat16 [8, 65536, 512], P('table', 'tm'), may hold values from -1.1953125 to 1.1953125
- bc_proj: bfloat16 [8, 65536, 128], P('table', 'tm'), may hold values from -0.18847656 to 0.18847656
- decay_log: float32 [8, 8, 65536], P('table', None, 'tm'), may hold values from -1 to 0
- skip_gain: float32 [8], replicated, may hold values from 0.5 to 1.5
- owner: int32 [8, 65536, 1], P('table', 'tm'), may hold values from 0 to 255; in each aligned block of 2048 rows (0 to 2047, 2048 to 4095, ..., all dimensions but the last counted through in order) at most 16 rows name the same one
- item_row: int32 [8, 65536], P('table', 'tm'), may hold values from 0 to 1535
- table: bfloat16 [393216, 512], P(('tm', 'table')), may hold values from -3 to 3
- accum: float32 [393216, 512], P(('tm', 'table')), may hold values from 1 to 10
Outputs:
- new_table: bfloat16 [393216, 512], P(('tm', 'table'))
- new_accum: float32 [393216, 512], P(('tm', 'table'))
Inputs may be any that keep to these rules, and one draw needn't show every extreme that they name: Among the events of one device at most 16 have the same owner; in every draw some device has exactly 16 events for some owner.
All inputs are finite; a program needn't handle non-finite values.
Results may differ from a plain program's by a relative error of at most 0.0018.
Values may be sent and summed in bfloat16 or wider, within the bound.
A program may use at most 128 MiB of HBM per device.

v0:
```python
import jax
import jax.numpy as jnp
from jax import lax
from jax.sharding import PartitionSpec as P

HEADS = 8
STATE = 64
GROUP = 256


learn_rate = 1.0


def entering(x, axis, combine, identity):
    size, mine = (lax.axis_size(axis), lax.axis_index(axis))
    everything = jax.tree.map(lambda part: lax.all_gather(part, axis), x)
    start = jax.tree.map(
        lambda part, zero: jnp.broadcast_to(jnp.asarray(zero, part.dtype), part.shape), x, identity
    )

    def hop(k, before):
        at = size - 1 - k
        reached = at > mine
        new = combine(before, jax.tree.map(lambda part: part[at], everything))
        return jax.tree.map(lambda a, b: jnp.where(reached, a, b), new, before)

    return lax.fori_loop(0, size, hop, start)


def block_end(grad_block, c_block, decay_block):
    cumul = jnp.cumsum(decay_block, axis=1)
    length = grad_block.shape[0]
    scaled = (
        grad_block.astype(jnp.float32).reshape(length, HEADS, -1) * jnp.exp(cumul).T[:, :, None]
    )
    ends = jnp.einsum(
        "thp,tn->hpn", scaled, c_block.astype(jnp.float32), precision=lax.Precision.HIGHEST
    )
    return (cumul[:, -1], ends)


def fold_back(carry, item):
    log_end, end_term = item
    return (end_term + jnp.exp(log_end)[..., None, None] * carry, carry)


def block_rows(grad_block, b_block, c_block, decay_block, carried, skip_gain):
    length = grad_block.shape[0]
    cumul = jnp.cumsum(decay_block, axis=1)
    scores = jnp.dot(c_block, b_block.T, preferred_element_type=jnp.float32)
    later = jnp.arange(length)[:, None] >= jnp.arange(length)[None, :]
    gaps = jnp.where(later[None], cumul[:, :, None] - cumul[:, None, :], 0.0)
    mixing = jnp.where(later[None], jnp.exp(gaps) * scores[None], 0.0).astype(jnp.bfloat16)
    heads_grad = grad_block.reshape(length, HEADS, -1)
    inner = jnp.einsum("hts,thp->shp", mixing, heads_grad, preferred_element_type=jnp.float32)
    fading = jnp.exp(cumul[:, -1:] - cumul)
    carried_part = (
        jnp.einsum(
            "hpn,sn->shp", carried, b_block.astype(jnp.float32), precision=lax.Precision.HIGHEST
        )
        * fading.T[:, :, None]
    )
    total = inner + carried_part + skip_gain[None, :, None] * heads_grad.astype(jnp.float32)
    return total.reshape(length, -1).astype(jnp.bfloat16)


def compose(earlier, later):
    return (earlier[0] + later[0], later[1] + jnp.exp(later[0])[..., None] * earlier[1])


def on_device(out_grad, bc_proj, decay_log, skip_gain, owner, item_row, table, accum):
    users, events, width = out_grad.shape
    blocks = events // GROUP
    head_dim = width // HEADS
    grad_blocks = out_grad.reshape(users * blocks, GROUP, width)
    b_blocks = bc_proj[:, :, :STATE].reshape(users * blocks, GROUP, STATE)
    c_blocks = bc_proj[:, :, STATE:].reshape(users * blocks, GROUP, STATE)
    decay_blocks = (
        decay_log.reshape(users, HEADS, blocks, GROUP)
        .transpose(0, 2, 1, 3)
        .reshape(users * blocks, HEADS, GROUP)
    )
    log_ends, end_terms = jax.vmap(block_end)(grad_blocks, c_blocks, decay_blocks)
    log_seq = log_ends.reshape(users, blocks, HEADS).transpose(1, 0, 2)
    end_seq = end_terms.reshape(users, blocks, HEADS, head_dim, STATE).transpose(1, 0, 2, 3, 4)
    empty = jnp.zeros((users, HEADS, head_dim, STATE), jnp.float32)
    device_end, _ = lax.scan(fold_back, empty, (log_seq, end_seq), reverse=True)
    device_log = jnp.sum(log_seq, axis=0)
    device_flat = device_end.reshape(users, HEADS, head_dim * STATE)
    identity = (
        jnp.zeros((users, HEADS), jnp.float32),
        jnp.zeros((users, HEADS, head_dim * STATE), jnp.float32),
    )
    _, incoming_flat = entering((device_log, device_flat), "tm", compose, identity)
    incoming = incoming_flat.reshape(users, HEADS, head_dim, STATE)
    _, carried_seq = lax.scan(fold_back, incoming, (log_seq, end_seq), reverse=True)
    carried = carried_seq.transpose(1, 0, 2, 3, 4).reshape(users * blocks, HEADS, head_dim, STATE)
    rows = jax.vmap(lambda a, b, c, d, e: block_rows(a, b, c, d, e, skip_gain))(
        grad_blocks, b_blocks, c_blocks, decay_blocks, carried
    )
    flat_rows = rows.reshape(users * events, width)
    target = owner.reshape(-1)
    local_row = item_row.reshape(-1)
    tm_count = lax.axis_size("tm")
    table_count = lax.axis_size("table")
    holders = tm_count * table_count
    capacity = max(2, 2 * users * events // holders)
    hits = (target[:, None] == jnp.arange(holders, dtype=jnp.int32)[None, :]).astype(jnp.int32)
    before = jnp.cumsum(hits, axis=0) - hits
    slot = jnp.sum(before * hits, axis=1)
    position = target * capacity + slot
    send_rows = jnp.zeros((holders * capacity, width), jnp.bfloat16).at[position].set(flat_rows)
    send_ids = jnp.zeros((holders * capacity,), jnp.int32).at[position].set(local_row)
    send_rows = send_rows.reshape(tm_count, table_count, capacity, width)
    send_ids = send_ids.reshape(tm_count, table_count, capacity)
    got_rows, got_ids = (
        lax.all_to_all(
            lax.all_to_all(send_rows, "tm", split_axis=0, concat_axis=0, tiled=True),
            "table",
            split_axis=1,
            concat_axis=1,
            tiled=True,
        ),
        lax.all_to_all(
            lax.all_to_all(send_ids, "tm", split_axis=0, concat_axis=0, tiled=True),
            "table",
            split_axis=1,
            concat_axis=1,
            tiled=True,
        ),
    )
    owned = table.shape[0]
    summed = jax.ops.segment_sum(
        got_rows.reshape(-1, width).astype(jnp.float32), got_ids.reshape(-1), num_segments=owned
    )
    new_accum = accum + summed * summed
    new_table = (table.astype(jnp.float32) - learn_rate * summed / jnp.sqrt(new_accum)).astype(
        jnp.bfloat16
    )
    return (new_table, new_accum)


def solution(mesh):
    placed = (
        P("table", "tm", None),
        P("table", "tm", None),
        P("table", None, "tm"),
        P(),
        P("table", "tm", None),
        P("table", "tm"),
        P(("tm", "table"), None),
        P(("tm", "table"), None),
    )
    return jax.shard_map(
        on_device,
        mesh=mesh,
        in_specs=placed,
        out_specs=(P(("tm", "table"), None), P(("tm", "table"), None)),
        check_vma=False,
    )
```

profile of v0, /device:TPU:8, one launch (start us, length us, event | category | flops | bytes accessed | tf_op | source)
XLA Modules:
  0.0 411.6 jit_solution(11137060329428828435)
XLA Ops:
  7.2 8.1 %reduce-window.16 = f32[8,8,2,128]{3,1,2,0:T(8,128)S(1)} reduce-window(f32[8,8,2,128]{3,1,2,0:T(8,128)} %bitcast.120, f32[]{:T(128)} %constant.139.clone.1), window={size=1x1x1x128 pad=0_0x0_0x0_0x127_0}, to_apply=%region_4.5 | reduce-window | flops 2080768 | bytes 131076 | tf_op jit(solution)/shard_map/reduce-window.2
  17.1 1.4 fusion.32
  18.5 3.7 reshape.223
  22.2 5.1 %copy.116 = bf16[8,256,8,64]{1,3,2,0:T(8,128)(2,1)} copy(bf16[8,256,8,64]{3,2,1,0:T(8,128)(2,1)} %reshape.223) | data formatting | bytes 4194304 | tf_op jit(solution)/shard_map/vmap()/reshape;reshape | solution.py:54
  27.3 3.8 fusion.24
  31.1 1.1 while.48
  33.4 1.3 copy-done
  34.8 1.8 broadcast_add_fusion
  36.7 1.2 copy.106
  39.5 8.2 %scatter_custom_fusion = s32[4096]{0:T(1024)S(1)} fusion(s32[2048]{0:T(1024)S(1)} %bitcast.125, s32[2048]{0:T(1024)} %bitcast.127, s32[]{:T(128)} %constant.140.clone.1), kind=kCustom, calls=%fused_computation.59 | custom fusion | bytes 16896 | tf_op jit(solution)/shard_map/scatter | solution.py:113
  48.5 11.7 %all-to-all-start = ((s32[32,1,128]{2,1,0:T(1,128)}), s32[32,1,128]{2,1,0:T(1,128)S(1)}, u32[]{:S(2)}, u32[]{:S(2)}) async-start(s32[32,1,128]{2,1,0:T(1,128)} %reshape.232), calls=%async_computation | async-start | bytes 32768 | tf_op jit(solution)/shard_map/all_to_all | solution.py:125
  61.8 71.0 %all-reduce = f32[256]{0:T(256)S(1)} all-reduce(f32[256]{0:T(256)S(1)} %dynamic-update-slice), channel_id=2, replica_groups=mesh['tm'=32,'table'=8] {'tm'}, use_global_device_ids=true, to_apply=%add | all-reduce | flops 256 | bytes 2048
  134.3 1.8 fusion.33
  136.1 33.4 %while.49 = (s32[]{:T(128)}, f32[1,8,4096]{2,1,0:T(8,128)S(1)}, s32[]{:T(128)}, f32[32,1,8,4096]{3,2,1,0:T(8,128)}, f32[32,1,8]{2,1,0:T(1,128)S(1)}, /*index=5*/s32[]{:T(128)}, s32[]{:T(128)}, s32[]{:T(128)}, s32[]{:T(128)}) while((s32[]{:T(128)}, f32[1,8,4096]{2,1,0:T(8,128)S(1)}, s32[]{:T(128)}, f32[32,1,8,4096]{3,2,1,0:T(8,128)}, ...), condition=%wide.region_10.11_spmd.clone, body=%wide.region_9.10_spmd.clone.sunk | while | flops 131080 | bytes 393479 | solution.py:27
  137.1 1.0 fusion.42
  138.2 1.0 fusion.42
  139.2 1.0 fusion.42
  141.3 1.0 fusion.42
  143.4 1.0 fusion.42
  144.4 1.0 fusion.42
  146.5 1.0 fusion.42
  148.6 1.0 fusion.42
  150.7 1.0 fusion.42
  152.8 1.0 fusion.42
  154.9 1.0 fusion.42
  157.0 1.0 fusion.42
  159.1 1.0 fusion.42
  161.2 1.0 fusion.42
  163.3 1.0 fusion.42
  164.3 1.0 fusion.42
  166.4 1.0 fusion.42
  168.5 1.0 fusion.42
  169.6 1.6 broadcast_in_dim.71
  171.2 11.9 %while.47 = (s32[]{:T(128)}, f32[1,8,64,64]{3,2,1,0:T(8,128)S(1)}, f32[8,1,8,64,64]{4,3,2,1,0:T(8,128)}, f32[8,1,8,64,64]{4,3,2,1,0:T(8,128)S(1)}, f32[8,1,8]{2,1,0:T(1,128)}, /*index=5*/s32[]{:T(128)}, s32[]{:T(128)}) while((s32[]{:T(128)}, f32[1,8,64,64]{3,2,1,0:T(8,128)S(1)}, f32[8,1,8,64,64]{4,3,2,1,0:T(8,128)}, ...), condition=%wide.region_12.13_spmd, body=%wide.region_11.12_spmd.sunk | while | flops 65539 | bytes 786629 | solution.py:96
  183.2 3.6 fusion.17
  186.8 5.3 %fusion.13 = bf16[8,256,8,64]{1,3,2,0:T(8,128)(2,1)S(1)} fusion(bf16[8,256,8,64]{1,3,2,0:T(8,128)(2,1)S(1)} %copy-done.1, f32[8,8,64,256]{3,2,1,0:T(8,128)S(1)} %fusion.17, f32[8,256,256]{2,1,0:T(8,128)S(1)} %copy-done.3, f32[8,8,256]{2,1,0:T(8,128)S(1)} %copy-done.6, pred[256,256]{1,0:T(8,128)(4,1)S(1)} %copy-done.8, f32[8]{0:T(128)S(1)} %copy-done.14, ...), kind=kOutput, calls=%fused_computation.27 | convolution fusion | flops 564133888 | bytes 10682400 | tf_op jit(solution)/shard_map/vmap(hts,thp->shp)/dot_general | solution.py:55
  192.1 3.6 copy.141
  195.8 5.4 %reshape.222 = bf16[2048,512]{1,0:T(8,128)(2,1)S(1)} reshape(bf16[8,256,8,64]{3,2,1,0:T(8,128)(2,1)} %copy.141) | data formatting | bytes 4194304 | tf_op jit(solution)/shard_map/vmap()/convert_element_type | solution.py:64
  201.2 12.3 %scatter_custom_fusion.1 = bf16[4096,512]{1,0:T(8,128)(2,1)} fusion(s32[2048]{0:T(1024)} %bitcast.126, bf16[2048,512]{1,0:T(8,128)(2,1)S(1)} %reshape.222, bf16[]{:T(256)} %constant.143.clone.1), kind=kCustom, calls=%fused_computation.38 | custom fusion | bytes 4194816 | tf_op jit(solution)/shard_map/scatter | solution.py:112
  213.4 9.3 %all-to-all-start.2 = ((bf16[32,8,16,512]{3,2,1,0:T(8,128)(2,1)}), bf16[32,8,16,512]{3,2,1,0:T(8,128)(2,1)}, u32[]{:S(2)}, u32[]{:S(2)}) async-start(bf16[32,8,16,512]{3,2,1,0:T(8,128)(2,1)} %bitcast.110), calls=%async_computation.2 | async-start | bytes 8388608 | tf_op jit(solution)/shard_map/all_to_all | solution.py:118
  224.9 79.4 %all-to-all-done.2 = bf16[32,8,16,512]{3,2,1,0:T(8,128)(2,1)} async-done(((bf16[32,8,16,512]{3,2,1,0:T(8,128)(2,1)}), bf16[32,8,16,512]{3,2,1,0:T(8,128)(2,1)}, u32[]{:S(2)}, u32[]{:S(2)}) %all-to-all-start.2) | async-done | bytes 4194336 | tf_op jit(solution)/shard_map/all_to_all | solution.py:118
  304.3 4.4 %all-to-all-start.1 = ((s32[8,1,512]{2,1,0:T(1,128)}), s32[8,1,512]{2,1,0:T(1,128)S(1)}, u32[]{:S(2)}, u32[]{:S(2)}) async-start(s32[8,1,512]{2,1,0:T(1,128)} %reshape.234), calls=%async_computation.1 | async-start | bytes 32768 | tf_op jit(solution)/shard_map/all_to_all | solution.py:124
  308.6 4.8 %copy.127 = bf16[32,8,16,512]{3,2,0,1:T(8,128)(2,1)} copy(bf16[32,8,16,512]{3,2,1,0:T(8,128)(2,1)} %all-to-all-done.2) | data formatting | bytes 8388608 | tf_op jit(solution)/shard_map/all_to_all | solution.py:118
  314.0 4.8 %all-to-all-start.3 = ((bf16[32,8,16,512]{3,2,0,1:T(8,128)(2,1)}), bf16[32,8,16,512]{3,2,0,1:T(8,128)(2,1)}, u32[]{:S(2)}, u32[]{:S(2)}) async-start(bf16[32,8,16,512]{3,2,0,1:T(8,128)(2,1)} %copy.127), calls=%async_computation.3 | async-start | bytes 8388608 | tf_op jit(solution)/shard_map/all_to_all | solution.py:117
  319.8 48.4 %all-to-all-done.3 = bf16[32,8,16,512]{3,2,0,1:T(8,128)(2,1)} async-done(((bf16[32,8,16,512]{3,2,0,1:T(8,128)(2,1)}), bf16[32,8,16,512]{3,2,0,1:T(8,128)(2,1)}, u32[]{:S(2)}, u32[]{:S(2)}) %all-to-all-start.3) | async-done | bytes 4194336 | tf_op jit(solution)/shard_map/all_to_all | solution.py:117
  368.2 4.8 %copy.128 = bf16[32,8,16,512]{3,2,1,0:T(8,128)(2,1)} copy(bf16[32,8,16,512]{3,2,0,1:T(8,128)(2,1)} %all-to-all-done.3) | data formatting | bytes 8388608 | tf_op jit(solution)/shard_map/all_to_all | solution.py:117
  373.0 26.3 %scatter_custom_fusion.2 = f32[1536,512]{1,0:T(8,128)S(1)} fusion(s32[4096]{0:T(1024)S(1)} %reshape.207, bf16[4096,512]{1,0:T(8,128)(2,1)} %bitcast.111, f32[]{:T(128)} %constant.139.clone.1), kind=kCustom, calls=%fused_computation.16 | custom fusion | flops 4194304 | bytes 7340036 | tf_op jit(solution)/shard_map/scatter-add | solution.py:133
  399.3 5.5 %subtract_convert_fusion = (bf16[1536,512]{1,0:T(8,128)(2,1)}, f32[1536,512]{1,0:T(8,128)}) fusion(f32[1536,512]{1,0:T(8,128)S(1)} %scatter_custom_fusion.2, bf16[1536,512]{1,0:T(8,128)(2,1)} %param.20, f32[1536,512]{1,0:T(8,128)} %param.21), kind=kLoop, calls=%fused_computation.30 | loop fusion | flops 4718592 | bytes 12582912 | tf_op jit(solution)/shard_map/convert_element_type | solution.py:137
  (157 shorter events, 38.3 us)
Async XLA Ops:
  7.2 11.3 %copy-start.2 = (bf16[1,2048,512]{2,1,0:T(8,128)(2,1)S(1)}, bf16[1,2048,512]{2,1,0:T(8,128)(2,1)}, u32[]{:S(2)}) copy-start(bf16[1,2048,512]{2,1,0:T(8,128)(2,1)} %param.14) | copy-start | bytes 6291460
  7.2 128.9 %all-gather.3.cloned.1.call-start = ((), (), s32[]{:S(2)}) async-start(), calls=%async_computation.4 | async-start | bytes 4325376 | tf_op jit(solution)/shard_map/all_gather | solution.py:16
  15.8 0.6 copy-start.4
  31.1 1.9 copy-start.7
  32.2 0.8 copy-start.10
  33.4 1.3 copy-start
  36.6 23.6 %copy-start.15 = (u32[256]{0:T(256)S(1)}, u32[256]{0:T(256)}, u32[]{:S(2)}) copy-start(u32[256]{0:T(256)} %constant.153) | copy-start | bytes 3076
  36.6 25.0 %copy-start.13 = (f32[8]{0:T(128)S(1)}, f32[8]{0:T(128)}, u32[]{:S(2)}) copy-start(f32[8]{0:T(128)} %get-tuple-element.436) | copy-start | bytes 100
  36.7 96.9 %copy-start.5 = (f32[8,8,256]{2,1,0:T(8,128)S(1)}, f32[8,8,256]{2,1,0:T(8,128)}, u32[]{:S(2)}) copy-start(f32[8,8,256]{2,1,0:T(8,128)} %copy-done.4) | copy-start | bytes 196612
  36.7 96.9 %copy-start.11 = (f32[8,1,8]{2,1,0:T(1,128)S(1)}, f32[8,1,8]{2,1,0:T(1,128)}, u32[]{:S(2)}) copy-start(f32[8,1,8]{2,1,0:T(1,128)} %copy-done.10) | copy-start | bytes 772
  38.9 0.6 copy-start.12
  48.5 164.9 %all-to-all-start = ((s32[32,1,128]{2,1,0:T(1,128)}), s32[32,1,128]{2,1,0:T(1,128)S(1)}, u32[]{:S(2)}, u32[]{:S(2)}) async-start(s32[32,1,128]{2,1,0:T(1,128)} %reshape.232), calls=%async_computation | async-start | bytes 32768 | tf_op jit(solution)/shard_map/all_to_all | solution.py:125
  183.1 3.7 copy-start.1
  183.1 3.7 copy-start.3
  183.1 3.7 copy-start.6
  183.1 3.7 copy-start.8
  183.1 3.7 copy-start.9
  183.1 3.7 copy-start.14
  213.4 90.9 %all-to-all-start.2 = ((bf16[32,8,16,512]{3,2,1,0:T(8,128)(2,1)}), bf16[32,8,16,512]{3,2,1,0:T(8,128)(2,1)}, u32[]{:S(2)}, u32[]{:S(2)}) async-start(bf16[32,8,16,512]{3,2,1,0:T(8,128)(2,1)} %bitcast.110), calls=%async_computation.2 | async-start | bytes 8388608 | tf_op jit(solution)/shard_map/all_to_all | solution.py:118
  304.3 9.7 %all-to-all-start.1 = ((s32[8,1,512]{2,1,0:T(1,128)}), s32[8,1,512]{2,1,0:T(1,128)S(1)}, u32[]{:S(2)}, u32[]{:S(2)}) async-start(s32[8,1,512]{2,1,0:T(1,128)} %reshape.234), calls=%async_computation.1 | async-start | bytes 32768 | tf_op jit(solution)/shard_map/all_to_all | solution.py:124
  314.0 54.2 %all-to-all-start.3 = ((bf16[32,8,16,512]{3,2,0,1:T(8,128)(2,1)}), bf16[32,8,16,512]{3,2,0,1:T(8,128)(2,1)}, u32[]{:S(2)}, u32[]{:S(2)}) async-start(bf16[32,8,16,512]{3,2,0,1:T(8,128)(2,1)} %copy.127), calls=%async_computation.3 | async-start | bytes 8388608 | tf_op jit(solution)/shard_map/all_to_all | solution.py:117
Sparse Core Ops, SparseCore 0:
  33.1 83.4 all-gather.2
where the time goes:
time: 414 us; the launch traced here: 412 us
  waiting for transfers between devices  128 us (31%)
  other arithmetic  80.1 us (19%)
  blocking collectives  71 us (17%)
  local copies, waits for them, and re-layouts  70.6 us (17%)
  starting transfers between devices  30.2 us (7%)
  between operations  15.2 us (4%)
  matrix products  14.5 us (4%)
    all_to_all x1, waiting for transfers between devices, on_device(): lax.all_to_all(send_rows, 'tm', split_axis=0, concat_axis=0, tiled=True)  79.4 us
    unnamed x1, blocking collectives  71 us
    all_to_all x1, waiting for transfers between devices, on_device(): lax.all_to_all(lax.all_to_all(send_rows, 'tm', split_axis=0, concat_axis=...  48.4 us
    select_n x32, other arithmetic, hop(): return jax.tree.map(lambda a, b: jnp.where(reached, a, b), new, before)  31.8 us
    scatter-add x1, other arithmetic, on_device(): jax.ops.segment_sum(got_rows.reshape(-1, width).astype(jnp.float32), got_...  26.3 us
    scatter x1, local copies, waits for them, and re-layouts, on_device(): jnp.zeros((holders * capacity, width), jnp.bfloat16).at[position]  12.3 us
    all_to_all x1, starting transfers between devices, on_device(): lax.all_to_all(send_ids, 'tm', split_axis=0, concat_axis=0, tiled=True)  11.7 us
    another operation x5, other arithmetic  10.4 us
  transfers between devices with their start and end apart: 5, of which 3 were waited for; matrix products, arithmetic and copies ran while one was open for 25% of the time, Pallas kernels for 0%

commit v1 on v0

v1 whole, which is shorter than its diff:
```python
import functools

import jax
import jax.numpy as jnp
from jax import lax
from jax.experimental import pallas as pl
from jax.experimental.pallas import tpu as pltpu
from jax.sharding import PartitionSpec as P

HEADS = 8
STATE = 64
GROUP = 256
CAP = 16
LANES = 128
RATE = 1.0
F32 = jnp.float32
BF16 = jnp.bfloat16


def dims(lhs, rhs):
    return (((lhs,), (rhs,)), ((), ()))


def spread(column, width):
    heads = lax.broadcasted_iota(jnp.int32, (HEADS, width), 0)
    owner = lax.broadcasted_iota(jnp.int32, (HEADS, width), 1) // (width // HEADS)
    pick = (heads == owner).astype(BF16)
    high = column.astype(BF16)
    low = (column - high.astype(F32)).astype(BF16)
    return jnp.dot(high, pick, preferred_element_type=F32) + jnp.dot(
        low, pick, preferred_element_type=F32
    )


def column_sums(decay):
    at = lax.broadcasted_iota(jnp.int32, (GROUP, GROUP), 0)
    before = lax.broadcasted_iota(jnp.int32, (GROUP, GROUP), 1)
    upto = (before <= at).astype(F32)
    return lax.dot_general(
        upto, decay, dims(1, 1), precision=lax.Precision.HIGHEST, preferred_element_type=F32
    )


def row_sums(decay):
    before = lax.broadcasted_iota(jnp.int32, (GROUP, GROUP), 0)
    at = lax.broadcasted_iota(jnp.int32, (GROUP, GROUP), 1)
    upto = (before <= at).astype(F32)
    return jnp.dot(decay, upto, precision=lax.Precision.HIGHEST, preferred_element_type=F32)


def route_kernel(owner_ref, row_ref, place_ref, ids_ref):
    holders = ids_ref.shape[0]
    blocks = owner_ref.shape[0]
    holder = lax.broadcasted_iota(jnp.int32, (holders, GROUP), 0)
    earlier = (
        lax.broadcasted_iota(jnp.int32, (GROUP, GROUP), 0)
        < lax.broadcasted_iota(jnp.int32, (GROUP, GROUP), 1)
    ).astype(BF16)
    slots = lax.broadcasted_iota(jnp.int32, (CAP, GROUP), 0)
    carry = jnp.zeros((holders, 1), F32)
    ids = jnp.zeros((holders, 2 * CAP), F32)
    for b in range(blocks):
        own = owner_ref[b : b + 1, :]
        hit = holder == own
        hits = jnp.where(hit, 1.0, 0.0).astype(F32)
        hits_low = hits.astype(BF16)
        before = jnp.dot(hits_low, earlier, preferred_element_type=F32) + carry
        slot = jnp.sum(hits * before, axis=0, keepdims=True).astype(jnp.int32)
        carry = carry + jnp.sum(hits, axis=1, keepdims=True)
        place_ref[b : b + 1, :] = own * CAP + slot
        mark = row_ref[b : b + 1, :] + 1
        high = lax.shift_right_logical(mark, 6)
        low = lax.bitwise_and(mark, 63)
        chosen = slots == slot
        table = jnp.concatenate(
            [
                jnp.where(chosen, high, 0).astype(F32),
                jnp.where(chosen, low, 0).astype(F32),
            ],
            axis=0,
        ).astype(BF16)
        ids = ids + lax.dot_general(hits_low, table, dims(1, 1), preferred_element_type=F32)
    total = ids[:, :CAP] * 64.0 + ids[:, CAP:] - 1.0
    ids_ref[...] = total.astype(jnp.int32)


def ends_kernel(grad_ref, bc_ref, decay_ref, ends_ref, fall_ref, send_ref, state, decayed):
    step = pl.program_id(0)
    width = grad_ref.shape[1]

    @pl.when(step == 0)
    def _():
        state[...] = jnp.zeros_like(state)
        decayed[...] = jnp.ones_like(decayed)

    factor = spread(jnp.exp(column_sums(decay_ref[...])), width)
    scaled = grad_ref[...].astype(F32) * factor
    high = scaled.astype(BF16)
    low = (scaled - high.astype(F32)).astype(BF16)
    c_turned = bc_ref[...].astype(F32).T[STATE:, :].astype(BF16)
    ends = jnp.dot(c_turned, high, preferred_element_type=F32) + jnp.dot(
        c_turned, low, preferred_element_type=F32
    )
    fall = factor[GROUP - 1 : GROUP, :]
    ends_ref[...] = ends
    fall_ref[...] = jnp.broadcast_to(fall, fall_ref.shape)
    state[...] = ends + fall * state[...]
    decayed[...] = decayed[...] * fall

    @pl.when(step == pl.num_programs(0) - 1)
    def _():
        tiles = width // LANES
        for r in range(STATE // 8):
            for j in range(tiles):
                lanes = slice(j * LANES, (j + 1) * LANES)
                send_ref[r * tiles + j, 0] = state[8 * r : 8 * r + 8, lanes]
                send_ref[r * tiles + j, 1] = decayed[:, lanes]


def within_kernel(grad_ref, bc_ref, decay_ref, skip_ref, out_ref):
    width = grad_ref.shape[1]
    head_dim = width // HEADS
    rows = row_sums(decay_ref[...])
    columns = column_sums(decay_ref[...])
    b_part = bc_ref[:, :STATE]
    c_part = bc_ref[:, STATE:]
    scores = lax.dot_general(b_part, c_part, dims(1, 1), preferred_element_type=F32)
    lane = lax.broadcasted_iota(jnp.int32, (GROUP, LANES), 1)
    source = lax.broadcasted_iota(jnp.int32, (GROUP, GROUP), 0)
    later = lax.broadcasted_iota(jnp.int32, (GROUP, GROUP), 1)
    keep = later >= source
    per_tile = LANES // head_dim
    for j in range(width // LANES):
        lanes = slice(j * LANES, (j + 1) * LANES)
        grad = grad_ref[:, lanes]
        total = None
        for i in range(per_tile):
            h = j * per_tile + i
            gaps = rows[h : h + 1, :] - columns[:, h : h + 1]
            mixing = (jnp.exp(jnp.where(keep, gaps, -1e30)) * scores).astype(BF16)
            part = jnp.dot(mixing, grad, preferred_element_type=F32)
            part = part + skip_ref[h] * grad.astype(F32)
            total = part if total is None else jnp.where(lane >= i * head_dim, part, total)
        out_ref[:, lanes] = total


def scan_kernel(got_ref, out_ref):
    count = got_ref.shape[0]
    held = jnp.zeros(out_ref.shape[1:], F32)
    for at in range(count - 1, -1, -1):
        out_ref[at] = held
        held = got_ref[at, 0] + got_ref[at, 1] * held


def rows_kernel(
    place_ref, part_ref, bc_ref, decay_ref, ends_ref, fall_ref, in_ref, out_ref, carried, flat, packed
):
    step = pl.program_id(0)
    last = pl.num_programs(0) - 1
    width = part_ref.shape[1]
    tiles = width // LANES

    @pl.when(step == 0)
    def _():
        packed[...] = jnp.zeros_like(packed)
        for r in range(STATE // 8):
            for j in range(tiles):
                carried[8 * r : 8 * r + 8, j * LANES : (j + 1) * LANES] = in_ref[r * tiles + j]

    sums = column_sums(decay_ref[...])
    fading = spread(jnp.exp(sums[GROUP - 1 : GROUP, :] - sums), width)
    held = carried[...]
    high = held.astype(BF16)
    low = (held - high.astype(F32)).astype(BF16)
    b_part = bc_ref[:, :STATE]
    product = jnp.dot(b_part, high, preferred_element_type=F32) + jnp.dot(
        b_part, low, preferred_element_type=F32
    )
    rows = (part_ref[...] + product * fading).astype(BF16).astype(F32)
    carried[...] = ends_ref[...] + fall_ref[0:1, :] * held
    for j in range(tiles):
        flat[pl.ds(j, GROUP, stride=tiles), :] = rows[:, j * LANES : (j + 1) * LANES]
    block = last - step

    def place(s, carry):
        for i in range(8):
            at = s * 8 + i
            to = place_ref[block, at]
            packed[pl.ds(pl.multiple_of(to * tiles, tiles), tiles), :] = flat[
                pl.ds(pl.multiple_of(at * tiles, tiles), tiles), :
            ]
        return carry

    lax.fori_loop(0, GROUP // 8, place, 0)

    @pl.when(step == last)
    def _():
        chunk = 256

        def put(c, carry):
            for j in range(tiles):
                start = c * chunk * tiles + j
                out_ref[pl.ds(pl.multiple_of(c * chunk, chunk), chunk), j * LANES : (j + 1) * LANES] = packed[
                    pl.ds(start, chunk, stride=tiles), :
                ].astype(BF16)
            return carry

        lax.fori_loop(0, out_ref.shape[0] // chunk, put, 0)


def update_kernel(ids_ref, rows_ref, table_ref, accum_ref, new_table_ref, new_accum_ref):
    tall = table_ref.shape[0]
    base = pl.program_id(0) * tall
    own = lax.broadcasted_iota(jnp.int32, (tall, ids_ref.shape[1]), 0) + base
    hits = jnp.where(own == ids_ref[...], 1.0, 0.0).astype(BF16)
    summed = jnp.dot(hits, rows_ref[...], preferred_element_type=F32)
    accum = accum_ref[...] + summed * summed
    new_accum_ref[...] = accum
    new_table_ref[...] = (
        table_ref[...].astype(F32) - RATE * summed / jnp.sqrt(accum)
    ).astype(BF16)


def on_device(out_grad, bc_proj, decay_log, skip_gain, owner, item_row, table, accum):
    users, events, width = out_grad.shape
    blocks = events // GROUP
    tm_count = lax.axis_size("tm")
    holders = tm_count * lax.axis_size("table")
    grad = out_grad.reshape(events, width)
    bc = bc_proj.reshape(events, 2 * STATE)
    decay = decay_log.reshape(HEADS, events)
    vmem = pl.BlockSpec(memory_space=pltpu.VMEM)
    smem = pl.BlockSpec(memory_space=pltpu.SMEM)

    places, ids = pl.pallas_call(
        route_kernel,
        name="route",
        out_shape=(
            jax.ShapeDtypeStruct((blocks, GROUP), jnp.int32),
            jax.ShapeDtypeStruct((holders, CAP), jnp.int32),
        ),
        in_specs=[vmem, vmem],
        out_specs=(vmem, vmem),
    )(owner.reshape(blocks, GROUP), item_row.reshape(blocks, GROUP))
    got_ids = lax.all_to_all(ids, ("tm", "table"), split_axis=0, concat_axis=0, tiled=True)

    def back(n, second=0):
        return lambda i: (blocks - 1 - i, 0)

    grad_spec = pl.BlockSpec((GROUP, width), lambda i: (blocks - 1 - i, 0))
    bc_spec = pl.BlockSpec((GROUP, 2 * STATE), lambda i: (blocks - 1 - i, 0))
    decay_spec = pl.BlockSpec((HEADS, GROUP), lambda i: (0, blocks - 1 - i))
    ends_spec = pl.BlockSpec((STATE, width), lambda i: (blocks - 1 - i, 0))
    fall_spec = pl.BlockSpec((8, width), lambda i: (blocks - 1 - i, 0))
    ends, falls, state = pl.pallas_call(
        ends_kernel,
        name="ends",
        grid=(blocks,),
        out_shape=(
            jax.ShapeDtypeStruct((blocks * STATE, width), F32),
            jax.ShapeDtypeStruct((blocks * 8, width), F32),
            jax.ShapeDtypeStruct((tm_count, 2, 8, LANES), F32),
        ),
        in_specs=[grad_spec, bc_spec, decay_spec],
        out_specs=(
            ends_spec,
            fall_spec,
            pl.BlockSpec((tm_count, 2, 8, LANES), lambda i: (0, 0, 0, 0)),
        ),
        scratch_shapes=[pltpu.VMEM((STATE, width), F32), pltpu.VMEM((8, width), F32)],
    )(grad, bc, decay)
    got_state = lax.all_to_all(state, "tm", split_axis=0, concat_axis=0, tiled=True)

    part = pl.pallas_call(
        within_kernel,
        name="within",
        grid=(blocks,),
        out_shape=jax.ShapeDtypeStruct((events, width), F32),
        in_specs=[grad_spec, bc_spec, decay_spec, smem],
        out_specs=grad_spec,
        cost_estimate=pl.CostEstimate(
            flops=2 * events * GROUP * (width * 2 + STATE),
            bytes_accessed=events * width * 6,
            transcendentals=events * GROUP * HEADS,
        ),
    )(grad, bc, decay, skip_gain)

    entering = pl.pallas_call(
        scan_kernel,
        name="scan",
        out_shape=jax.ShapeDtypeStruct((tm_count, 8, LANES), F32),
        in_specs=[vmem],
        out_specs=vmem,
    )(got_state)
    incoming = lax.all_to_all(entering, "tm", split_axis=0, concat_axis=0, tiled=True)

    slots = holders * CAP
    tiles = width // LANES
    send = pl.pallas_call(
        rows_kernel,
        name="rows",
        grid=(blocks,),
        out_shape=jax.ShapeDtypeStruct((slots, width), BF16),
        in_specs=[
            smem,
            grad_spec,
            bc_spec,
            decay_spec,
            ends_spec,
            fall_spec,
            pl.BlockSpec((tm_count, 8, LANES), lambda i: (0, 0, 0)),
        ],
        out_specs=pl.BlockSpec((slots, width), lambda i: (0, 0)),
        scratch_shapes=[
            pltpu.VMEM((STATE, width), F32),
            pltpu.VMEM((GROUP * tiles, LANES), F32),
            pltpu.VMEM((slots * tiles, LANES), F32),
        ],
    )(places, part, bc, decay, ends, falls, incoming)

    got = lax.all_to_all(
        send.reshape(holders, CAP, width), ("tm", "table"), split_axis=0, concat_axis=0, tiled=True
    )

    owned = table.shape[0]
    tall = 256
    tile = pl.BlockSpec((tall, width), lambda i: (i, 0))
    return pl.pallas_call(
        update_kernel,
        name="update",
        grid=(owned // tall,),
        out_shape=(
            jax.ShapeDtypeStruct((owned, width), BF16),
            jax.ShapeDtypeStruct((owned, width), F32),
        ),
        in_specs=[
            pl.BlockSpec((1, slots), lambda i: (0, 0)),
            pl.BlockSpec((slots, width), lambda i: (0, 0)),
            tile,
            tile,
        ],
        out_specs=(tile, tile),
    )(got_ids.reshape(1, slots), got.reshape(slots, width), table, accum)


def solution(mesh):
    placed = (
        P("table", "tm", None),
        P("table", "tm", None),
        P("table", None, "tm"),
        P(),
        P("table", "tm", None),
        P("table", "tm"),
        P(("tm", "table"), None),
        P(("tm", "table"), None),
    )
    return jax.shard_map(
        on_device,
        mesh=mesh,
        in_specs=placed,
        out_specs=(P(("tm", "table"), None), P(("tm", "table"), None)),
        check_vma=False,
    )
```

time: 414 us -> 217 us (0.52)
  other arithmetic: 80.1 us -> 2.27 us
  local copies, waits for them, and re-layouts: 70.6 us -> 2.47 us
  Pallas kernels: 0 us -> 59 us
  blocking collectives: 71 us -> 23 us
  waiting for transfers between devices: 128 us -> 98.8 us
  matrix products: 14.5 us -> 0 us
  between operations: 15.2 us -> 0.7 us
    unnamed x1 -> x0, blocking collectives: 71 us -> none
    pallas_call x0 -> x6, Pallas kernels: none -> 59 us  [the longest x1 21 us: on_device(): pl.pallas_call(rows_kernel, name='rows', grid=(blocks,), out_shape=jax.Sh...]
    select_n x33 -> x0, other arithmetic: 31.8 us -> none  [the longest x32 31.8 us: hop(): return jax.tree.map(lambda a, b: jnp.where(reached, a, b), new, before)]
    all_to_all x4 -> x3, waiting for transfers between devices: 128 us -> 98.8 us  [the longest x1 95.7 us: on_device(): lax.all_to_all(send.reshape(holders, CAP, width), ('tm', 'table'), split_...]
    scatter-add x1 -> x0, other arithmetic: 26.3 us -> none  [on_device(): jax.ops.segment_sum(got_rows.reshape(-1, width).astype(jnp.float32), got_...]
    all_to_all x0 -> x1, blocking collectives: none -> 23 us  [on_device(): lax.all_to_all(state, 'tm', split_axis=0, concat_axis=0, tiled=True)]
    scatter x2 -> x0, local copies, waits for them, and re-layouts: 20.5 us -> none  [the longest x1 12.3 us: on_device(): jnp.zeros((holders * capacity, width), jnp.bfloat16).at[position]]
    dot_general x4 -> x0, matrix products: 14.5 us -> none  [the longest x1 5.27 us: block_rows(): jnp.einsum('hts,thp->shp', mixing, heads_grad, preferred_element_type=jnp...]
  transfers between devices with their start and end apart: 5 -> 3, of which waited for: 3 -> 2; matrix products, arithmetic and copies ran while one was open for 25% -> 2% of each run, Pallas kernels for 0% -> 16%
where the time goes in v1:
time: 217 us; the launch traced here: 216 us
  waiting for transfers between devices  98.8 us (46%)
  Pallas kernels  59 us (27%)
  starting transfers between devices  29.8 us (14%)
  blocking collectives  23 us (11%)
  local copies, waits for them, and re-layouts  2.47 us (1%)
  other arithmetic  2.27 us (1%)
    all_to_all x1, waiting for transfers between devices, on_device(): lax.all_to_all(send.reshape(holders, CAP, width), ('tm', 'table'), split_...  95.7 us
    all_to_all x1, blocking collectives, on_device(): lax.all_to_all(state, 'tm', split_axis=0, concat_axis=0, tiled=True)  23 us
    pallas_call x1, Pallas kernels, on_device(): pl.pallas_call(rows_kernel, name='rows', grid=(blocks,), out_shape=jax.Sh...  21 us
    all_to_all x1, starting transfers between devices, on_device(): lax.all_to_all(send.reshape(holders, CAP, width), ('tm', 'table'), split_...  14.7 us
    pallas_call x1, Pallas kernels, on_device(): pl.pallas_call(update_kernel, name='update', grid=(owned // tall,), out_s...  12.1 us
    pallas_call x1, Pallas kernels, on_device(): pl.pallas_call(within_kernel, name='within', grid=(blocks,), out_shape=ja...  10.9 us
    pallas_call x1, Pallas kernels, on_device(): pl.pallas_call(ends_kernel, name='ends', grid=(blocks,), out_shape=(jax.S...  10.6 us
    all_to_all x1, starting transfers between devices, on_device(): lax.all_to_all(ids, ('tm', 'table'), split_axis=0, concat_axis=0, tiled=T...  9.54 us
  transfers between devices with their start and end apart: 3, of which 2 were waited for; matrix products, arithmetic and copies ran while one was open for 2% of the time, Pallas kernels for 16%

profile of v1, /device:TPU:8, one launch (start us, length us, event | category | flops | bytes accessed | tf_op | source)
XLA Modules:
  0.0 216.2 jit_solution(2947053955337086755)
XLA Ops:
  0.6 0.0 copy-start.1
  0.6 0.0 copy-start.2
  0.6 10.6 %ends.1 = (f32[512,512]{1,0:T(8,128)}, f32[64,512]{1,0:T(8,128)}, f32[32,2,8,128]{3,2,1,0:T(8,128)}) custom-call(bf16[2048,512]{1,0:T(8,128)(2,1)} %bitcast.10, bf16[2048,128]{1,0:T(8,128)(2,1)} %bitcast.12, f32[8,2048]{1,0:T(8,128)} %bitcast.15), custom_call_target="tpu_custom_call" | custom-call | tf_op jit(solution)/shard_map/ends/pallas_call | solution.py:255
  11.2 23.0 %all_to_all.24.got_ref = f32[32,2,8,128]{3,2,1,0:T(8,128)} all-to-all(f32[32,2,8,128]{3,2,1,0:T(8,128)} %get-tuple-element.11), channel_id=1, replica_groups=mesh['tm'=32,'table'=8] {'tm'}, dimensions={0} | all-to-all | bytes 524288 | tf_op jit(solution)/shard_map/all_to_all | solution.py:272
  34.3 1.7 scan.1
  35.9 5.6 %all-to-all-start.2 = ((f32[32,8,128]{2,1,0:T(8,128)}), f32[32,8,128]{2,1,0:T(8,128)S(1)}, u32[]{:S(2)}, u32[]{:S(2)}) async-start(f32[32,8,128]{2,1,0:T(8,128)} %scan.1), calls=%async_computation.2 | async-start | bytes 262144 | tf_op jit(solution)/shard_map/all_to_all | solution.py:295
  41.5 0.5 broadcast.9
  42.1 0.0 copy-done.1
  42.1 0.7 reduce.9
  42.7 0.6 reshape.31.owner_ref
  43.3 0.0 copy-done.2
  43.3 0.7 reduce.10
  44.0 0.6 reshape.32.row_ref
  44.6 2.7 %route.1 = (s32[8,256]{1,0:T(8,128)}, s32[256,16]{1,0:T(8,128)}) custom-call(s32[8,256]{1,0:T(8,128)} %reshape.31.owner_ref, s32[8,256]{1,0:T(8,128)} %reshape.32.row_ref), custom_call_target="tpu_custom_call" | custom-call | tf_op jit(solution)/shard_map/route/pallas_call | solution.py:235
  47.3 3.1 %all-to-all-done.2.in_ref = f32[32,8,128]{2,1,0:T(8,128)S(1)} async-done(((f32[32,8,128]{2,1,0:T(8,128)}), f32[32,8,128]{2,1,0:T(8,128)S(1)}, u32[]{:S(2)}, u32[]{:S(2)}) %all-to-all-start.2) | async-done | bytes 131104 | tf_op jit(solution)/shard_map/all_to_all | solution.py:295
  50.5 0.0 copy-start
  50.5 9.5 %all-to-all-start = ((s32[256,1,16]{2,1,0:T(1,128)}), s32[256,1,16]{2,1,0:T(1,128)S(1)}, u32[]{:S(2)}, u32[]{:S(2)}) async-start(s32[256,1,16]{2,1,0:T(1,128)} %bitcast.18), calls=%async_computation | async-start | bytes 262144 | tf_op jit(solution)/shard_map/all_to_all | solution.py:245
  60.0 10.9 %within.1.part_ref = f32[2048,512]{1,0:T(8,128)} custom-call(bf16[2048,512]{1,0:T(8,128)(2,1)} %bitcast.11, bf16[2048,128]{1,0:T(8,128)(2,1)} %bitcast.13, f32[8,2048]{1,0:T(8,128)} %bitcast.16, f32[8]{0:T(128)} %skip_ref.1), custom_call_target="tpu_custom_call" | custom-call | flops 1140850688 | bytes 6291456 | tf_op jit(solution)/shard_map/within/pallas_call | solution.py:274
  70.9 0.0 copy-done
  70.9 21.0 %rows.1 = bf16[4096,512]{1,0:T(8,128)(2,1)} custom-call(s32[8,256]{1,0:T(8,128)} %get-tuple-element.8.place_ref, f32[2048,512]{1,0:T(8,128)} %within.1.part_ref, bf16[2048,128]{1,0:T(8,128)(2,1)} %bitcast.14, f32[8,2048]{1,0:T(8,128)} %bitcast.17, f32[512,512]{1,0:T(8,128)} %get-tuple-element.9.ends_ref, f32[64,512]{1,0:T(8,128)} %get-tuple-element.10.fall_ref, ...), custom_call_target="tpu_custom_call" | custom-call | tf_op jit(solution)/shard_map/rows/pallas_call | solution.py:299
  92.0 0.0 all-to-all-done
  92.0 14.7 %all-to-all-start.3 = ((bf16[256,16,512]{2,1,0:T(8,128)(2,1)}), bf16[256,16,512]{2,1,0:T(8,128)(2,1)}, u32[]{:S(2)}, u32[]{:S(2)}) async-start(bf16[256,16,512]{2,1,0:T(8,128)(2,1)} %bitcast.9), calls=%async_computation.3 | async-start | bytes 8388608 | tf_op jit(solution)/shard_map/all_to_all | solution.py:321
  106.7 1.0 reduce.11
  107.7 0.7 reshape.33.ids_ref
  108.4 95.7 %all-to-all-done.3 = bf16[256,16,512]{2,1,0:T(8,128)(2,1)} async-done(((bf16[256,16,512]{2,1,0:T(8,128)(2,1)}), bf16[256,16,512]{2,1,0:T(8,128)(2,1)}, u32[]{:S(2)}, u32[]{:S(2)}) %all-to-all-start.3) | async-done | bytes 4194336 | tf_op jit(solution)/shard_map/all_to_all | solution.py:321
  204.1 12.1 %update.1 = (bf16[1536,512]{1,0:T(8,128)(2,1)}, f32[1536,512]{1,0:T(8,128)}) custom-call(s32[1,4096]{1,0:T(1,128)} %reshape.33.ids_ref, bf16[4096,512]{1,0:T(8,128)(2,1)} %bitcast.6.rows_ref, bf16[1536,512]{1,0:T(8,128)(2,1)} %table_ref.1, f32[1536,512]{1,0:T(8,128)} %accum_ref.1), custom_call_target="tpu_custom_call" | custom-call | tf_op jit(solution)/shard_map/update/pallas_call | solution.py:328
Async XLA Ops:
  0.6 41.4 %copy-start.1 = (s32[1,2048,1]{1,2,0:T(1,128)S(1)}, s32[1,2048,1]{1,2,0:T(1,128)}, u32[]{:S(2)}) copy-start(s32[1,2048,1]{1,2,0:T(1,128)} %param.12) | copy-start | bytes 24580
  0.6 42.7 %copy-start.2 = (s32[1,2048]{1,0:T(1,128)S(1)}, s32[1,2048]{1,0:T(1,128)}, u32[]{:S(2)}) copy-start(s32[1,2048]{1,0:T(1,128)} %param.13) | copy-start | bytes 24580
  35.9 14.5 %all-to-all-start.2 = ((f32[32,8,128]{2,1,0:T(8,128)}), f32[32,8,128]{2,1,0:T(8,128)S(1)}, u32[]{:S(2)}, u32[]{:S(2)}) async-start(f32[32,8,128]{2,1,0:T(8,128)} %scan.1), calls=%async_computation.2 | async-start | bytes 262144 | tf_op jit(solution)/shard_map/all_to_all | solution.py:295
  50.5 20.5 %copy-start = (f32[32,8,128]{2,1,0:T(8,128)}, f32[32,8,128]{2,1,0:T(8,128)S(1)}, u32[]{:S(2)}) copy-start(f32[32,8,128]{2,1,0:T(8,128)S(1)} %all-to-all-done.2.in_ref) | copy-start | bytes 393220
  50.5 41.5 %all-to-all-start = ((s32[256,1,16]{2,1,0:T(1,128)}), s32[256,1,16]{2,1,0:T(1,128)S(1)}, u32[]{:S(2)}, u32[]{:S(2)}) async-start(s32[256,1,16]{2,1,0:T(1,128)} %bitcast.18), calls=%async_computation | async-start | bytes 262144 | tf_op jit(solution)/shard_map/all_to_all | solution.py:245
  92.0 112.1 %all-to-all-start.3 = ((bf16[256,16,512]{2,1,0:T(8,128)(2,1)}), bf16[256,16,512]{2,1,0:T(8,128)(2,1)}, u32[]{:S(2)}, u32[]{:S(2)}) async-start(bf16[256,16,512]{2,1,0:T(8,128)(2,1)} %bitcast.9), calls=%async_computation.3 | async-start | bytes 8388608 | tf_op jit(solution)/shard_map/all_to_all | solution.py:321

commit v2 on v0

v2 whole, which is shorter than its diff:
```python
import functools

import jax
import jax.numpy as jnp
from jax import lax
from jax.experimental import pallas as pl
from jax.experimental.pallas import tpu as pltpu
from jax.sharding import PartitionSpec as P

HEADS = 8
STATE = 64
GROUP = 256
CAP = 16
LANES = 128
RATE = 1.0
F32 = jnp.float32
BF16 = jnp.bfloat16


def dims(lhs, rhs):
    return (((lhs,), (rhs,)), ((), ()))


MESH = pl.DeviceIdType.MESH


def spread(column, width):
    heads = lax.rem(lax.broadcasted_iota(jnp.int32, (2 * HEADS, width), 0), HEADS)
    owner = lax.broadcasted_iota(jnp.int32, (2 * HEADS, width), 1) // (width // HEADS)
    pick = jnp.where(heads == owner, 1.0, 0.0).astype(BF16)
    high = column.astype(BF16).astype(F32)
    both = jnp.concatenate([high, column - high], axis=1).astype(BF16)
    return jnp.dot(both, pick, preferred_element_type=F32)


def split(value, axis):
    high = value.astype(BF16)
    low = (value - high.astype(F32)).astype(BF16)
    return jnp.concatenate([high, low], axis=axis)


def route(owner_ref, row_ref, place_ref, holders):
    blocks = owner_ref.shape[1] // GROUP
    holder = lax.broadcasted_iota(jnp.int32, (holders, GROUP), 0)
    earlier = jnp.where(
        lax.broadcasted_iota(jnp.int32, (GROUP, GROUP), 0)
        < lax.broadcasted_iota(jnp.int32, (GROUP, GROUP), 1),
        1.0,
        0.0,
    ).astype(BF16)
    slots = lax.broadcasted_iota(jnp.int32, (LANES, GROUP), 0)
    carry = jnp.zeros((holders, 1), F32)
    ids = jnp.zeros((holders, LANES), F32)
    for b in range(blocks):
        part = slice(b * GROUP, (b + 1) * GROUP)
        own = owner_ref[:, part]
        hits = jnp.where(holder == own, 1.0, 0.0)
        hits_low = hits.astype(BF16)
        before = jnp.dot(hits_low, earlier, preferred_element_type=F32) + carry
        slot = jnp.sum(hits * before, axis=0, keepdims=True).astype(jnp.int32)
        carry = carry + jnp.sum(hits, axis=1, keepdims=True)
        place_ref[b : b + 1, :] = own * CAP + slot
        mark = row_ref[:, part] + 1
        chosen = slots == slot
        high = jnp.where(chosen, lax.shift_right_logical(mark, 6).astype(F32), 0.0).astype(BF16)
        low = jnp.where(chosen, lax.bitwise_and(mark, 63).astype(F32), 0.0).astype(BF16)
        ids = ids + 64.0 * lax.dot_general(
            hits_low, high, dims(1, 1), preferred_element_type=F32
        )
        ids = ids + lax.dot_general(hits_low, low, dims(1, 1), preferred_element_type=F32)
    return ids - 1.0


def front_kernel(
    tm_count,
    table_count,
    owner_ref,
    row_ref,
    grad_ref,
    bc_ref,
    decay_ref,
    skip_ref,
    flat_ref,
    place_ref,
    ids_ref,
    columns,
    sums,
    ends,
    falls,
    part,
    state,
    decayed,
    send,
    got,
    entering,
    incoming,
    ids_send,
    ids_got,
    send_sems,
    recv_sems,
    back_send_sems,
    back_recv_sems,
    ids_send_sems,
    ids_recv_sems,
):
    tm, tb = lax.axis_index("tm"), lax.axis_index("table")
    events, width = grad_ref.shape
    blocks = events // GROUP
    head_dim = width // HEADS
    tiles = width // LANES
    per_tile = LANES // head_dim

    barrier = pltpu.get_barrier_semaphore()

    def greet_tm(d, carry):
        pl.semaphore_signal(
            barrier, inc=1, device_id=(lax.rem(tm + d, tm_count), tb), device_id_type=MESH
        )
        return carry

    def greet_table(d, carry):
        pl.semaphore_signal(
            barrier, inc=1, device_id=(tm, lax.rem(tb + d, table_count)), device_id_type=MESH
        )
        return carry

    lax.fori_loop(1, tm_count, greet_tm, 0)
    lax.fori_loop(1, table_count, greet_table, 0)

    upto = jnp.where(
        lax.broadcasted_iota(jnp.int32, (GROUP, GROUP), 0)
        <= lax.broadcasted_iota(jnp.int32, (GROUP, GROUP), 1),
        1.0,
        0.0,
    )
    decays = jnp.concatenate(
        [decay_ref[:, b * GROUP : (b + 1) * GROUP] for b in range(blocks)], axis=0
    )
    running = jnp.dot(decays, upto, precision=lax.Precision.HIGHEST, preferred_element_type=F32)
    sums[...] = running
    for b in range(blocks):
        columns[b * GROUP : (b + 1) * GROUP, :] = running[b * HEADS : (b + 1) * HEADS, :].T

    state[...] = jnp.zeros_like(state)
    decayed[...] = jnp.ones_like(decayed)

    def block_at(b, tall):
        return pl.ds(pl.multiple_of(b * tall, tall), tall)

    def end(i, carry):
        b = blocks - 1 - i
        here = block_at(b, GROUP)
        factor = spread(jnp.exp(columns[here, :]), width)
        scaled = grad_ref[here, :].astype(F32) * factor
        high = scaled.astype(BF16)
        low = (scaled - high.astype(F32)).astype(BF16)
        c_turned = bc_ref[here, :].astype(F32).T[STATE:, :].astype(BF16)
        term = jnp.dot(c_turned, high, preferred_element_type=F32) + jnp.dot(
            c_turned, low, preferred_element_type=F32
        )
        fall = factor[GROUP - 1 : GROUP, :]
        ends[block_at(b, STATE), :] = term
        falls[block_at(b, 8), :] = jnp.broadcast_to(fall, (8, width))
        state[...] = term + fall * state[...]
        decayed[...] = decayed[...] * fall
        return carry

    lax.fori_loop(0, blocks, end, 0)
    for r in range(STATE // 8):
        for j in range(tiles):
            lanes = slice(j * LANES, (j + 1) * LANES)
            send[r * tiles + j, 0] = state[8 * r : 8 * r + 8, lanes]
            send[r * tiles + j, 1] = decayed[:, lanes]
    ids = route(owner_ref, row_ref, place_ref, tm_count * table_count)
    send[:, 2] = ids.reshape(tm_count, table_count, LANES)

    pl.semaphore_wait(barrier, tm_count + table_count - 2)

    def outward(d):
        to = lax.rem(tm + d, tm_count)
        return pltpu.make_async_remote_copy(
            src_ref=send.at[to],
            dst_ref=got.at[tm],
            send_sem=send_sems.at[d],
            recv_sem=recv_sems.at[d],
            device_id=(to, tb),
            device_id_type=MESH,
        )

    def backward(d):
        to = lax.rem(tm + d, tm_count)
        return pltpu.make_async_remote_copy(
            src_ref=entering.at[to],
            dst_ref=incoming.at[tm],
            send_sem=back_send_sems.at[d],
            recv_sem=back_recv_sems.at[d],
            device_id=(to, tb),
            device_id_type=MESH,
        )

    def sideways(d):
        to = lax.rem(tb + d, table_count)
        return pltpu.make_async_remote_copy(
            src_ref=ids_send.at[to],
            dst_ref=ids_got.at[tb],
            send_sem=ids_send_sems.at[d],
            recv_sem=ids_recv_sems.at[d],
            device_id=(tm, to),
            device_id_type=MESH,
        )

    def each(count, act):
        def body(d, carry):
            act(d)
            return carry

        lax.fori_loop(1, count, body, 0)

    each(tm_count, lambda d: outward(d).start())
    got[tm] = send[tm]

    lane = lax.broadcasted_iota(jnp.int32, (GROUP, LANES), 1)
    keep = lax.broadcasted_iota(jnp.int32, (GROUP, GROUP), 1) >= lax.broadcasted_iota(
        jnp.int32, (GROUP, GROUP), 0
    )

    def within(i, carry):
        b = blocks - 1 - i
        here = block_at(b, GROUP)
        rows = sums[block_at(b, HEADS), :]
        column = columns[here, :]
        scores = lax.dot_general(
            bc_ref[here, :STATE], bc_ref[here, STATE:], dims(1, 1), preferred_element_type=F32
        )
        for j in range(tiles):
            lanes = slice(j * LANES, (j + 1) * LANES)
            grad = grad_ref[here, lanes]
            total = None
            for k in range(per_tile):
                h = j * per_tile + k
                gaps = rows[h : h + 1, :] - column[:, h : h + 1]
                mixing = (jnp.exp(jnp.where(keep, gaps, -1e30)) * scores).astype(BF16)
                term = jnp.dot(mixing, grad, preferred_element_type=F32)
                term = term + skip_ref[h] * grad.astype(F32)
                total = term if total is None else jnp.where(lane >= k * head_dim, term, total)
            part[here, lanes] = total
        return carry

    first = blocks * 5 // 8
    lax.fori_loop(0, first, within, 0)

    each(tm_count, lambda d: outward(d).wait_recv())
    held = jnp.zeros((8, LANES), F32)
    for at in range(tm_count - 1, -1, -1):
        entering[at] = held
        held = got[at, 0] + got[at, 1] * held
    each(tm_count, lambda d: backward(d).start())
    incoming[tm] = entering[tm]
    for w in range(table_count):
        ids_send[w] = got[:, 2, w, :]
    each(table_count, lambda d: sideways(d).start())
    ids_got[tb] = ids_send[tb]

    lax.fori_loop(first, blocks, within, 0)

    each(tm_count, lambda d: backward(d).wait_recv())
    for r in range(STATE // 8):
        for j in range(tiles):
            state[8 * r : 8 * r + 8, j * LANES : (j + 1) * LANES] = incoming[r * tiles + j]

    def finish(i, carry):
        b = blocks - 1 - i
        here = block_at(b, GROUP)
        column = columns[here, :]
        fading = spread(jnp.exp(column[GROUP - 1 : GROUP, :] - column), width)
        carried = state[...]
        b_part = bc_ref[here, :STATE]
        product = jnp.dot(
            jnp.concatenate([b_part, b_part], axis=1),
            split(carried, 0),
            preferred_element_type=F32,
        )
        rows = (part[here, :] + product * fading).astype(BF16).astype(F32)
        fall = falls[block_at(b, 8), :]
        state[...] = ends[block_at(b, STATE), :] + fall[0:1, :] * carried
        for j in range(tiles):
            flat_ref[pl.ds(b * GROUP * tiles + j, GROUP, stride=tiles), :] = rows[
                :, j * LANES : (j + 1) * LANES
            ]
        return carry

    lax.fori_loop(0, blocks, finish, 0)
    each(table_count, lambda d: sideways(d).wait_recv())
    ids_ref[...] = ids_got[...]
    each(tm_count, lambda d: outward(d).wait_send())
    each(tm_count, lambda d: backward(d).wait_send())
    each(table_count, lambda d: sideways(d).wait_send())


def pack_kernel(place_ref, flat_ref, out_ref, packed):
    step = pl.program_id(0)
    tiles = out_ref.shape[1] // LANES

    @pl.when(step == 0)
    def _():
        packed[...] = jnp.zeros_like(packed)

    unroll = 16

    def place(s, carry):
        first = s * unroll
        to = [place_ref[step, first + i] for i in range(unroll)]
        rows = [
            flat_ref[pl.ds(pl.multiple_of((first + i) * tiles, tiles), tiles), :]
            for i in range(unroll)
        ]
        for i in range(unroll):
            packed[pl.ds(pl.multiple_of(to[i] * tiles, tiles), tiles), :] = rows[i]
        return carry

    lax.fori_loop(0, GROUP // unroll, place, 0)

    @pl.when(step == pl.num_programs(0) - 1)
    def _():
        chunk = 256

        def put(c, carry):
            for j in range(tiles):
                out_ref[
                    pl.ds(pl.multiple_of(c * chunk, chunk), chunk), j * LANES : (j + 1) * LANES
                ] = packed[pl.ds(c * chunk * tiles + j, chunk, stride=tiles), :].astype(BF16)
            return carry

        lax.fori_loop(0, out_ref.shape[0] // chunk, put, 0)


def update_kernel(ids_ref, rows_ref, table_ref, accum_ref, new_table_ref, new_accum_ref):
    tall = table_ref.shape[0]
    base = pl.program_id(0) * tall
    own = lax.broadcasted_iota(jnp.int32, (tall, ids_ref.shape[1]), 0) + base
    hits = jnp.where(own == ids_ref[...], 1.0, 0.0).astype(BF16)
    summed = jnp.dot(hits, rows_ref[...], preferred_element_type=F32)
    accum = accum_ref[...] + summed * summed
    new_accum_ref[...] = accum
    new_table_ref[...] = (
        table_ref[...].astype(F32) - RATE * summed / jnp.sqrt(accum)
    ).astype(BF16)


def on_device(out_grad, bc_proj, decay_log, skip_gain, owner, item_row, table, accum):
    users, events, width = out_grad.shape
    blocks = events // GROUP
    tiles = width // LANES
    tm_count = lax.axis_size("tm")
    table_count = lax.axis_size("table")
    holders = tm_count * table_count
    slots = holders * CAP
    vmem = pl.BlockSpec(memory_space=pltpu.VMEM)
    smem = pl.BlockSpec(memory_space=pltpu.SMEM)
    slices = (tm_count, 8, LANES)
    dma = pltpu.SemaphoreType.DMA

    flat, places, ids = pl.pallas_call(
        functools.partial(front_kernel, tm_count, table_count),
        name="front",
        out_shape=(
            jax.ShapeDtypeStruct((events * tiles, LANES), F32),
            jax.ShapeDtypeStruct((blocks, GROUP), jnp.int32),
            jax.ShapeDtypeStruct((table_count, tm_count, LANES), F32),
        ),
        in_specs=[vmem, vmem, vmem, vmem, vmem, smem],
        out_specs=(vmem, vmem, vmem),
        scratch_shapes=[
            pltpu.VMEM((events, HEADS), F32),
            pltpu.VMEM((blocks * HEADS, GROUP), F32),
            pltpu.VMEM((blocks * STATE, width), F32),
            pltpu.VMEM((blocks * 8, width), F32),
            pltpu.VMEM((events, width), F32),
            pltpu.VMEM((STATE, width), F32),
            pltpu.VMEM((8, width), F32),
            pltpu.VMEM((tm_count, 3, 8, LANES), F32),
            pltpu.VMEM((tm_count, 3, 8, LANES), F32),
            pltpu.VMEM(slices, F32),
            pltpu.VMEM(slices, F32),
            pltpu.VMEM((table_count, tm_count, LANES), F32),
            pltpu.VMEM((table_count, tm_count, LANES), F32),
            dma((tm_count,)),
            dma((tm_count,)),
            dma((tm_count,)),
            dma((tm_count,)),
            dma((table_count,)),
            dma((table_count,)),
        ],
        compiler_params=pltpu.CompilerParams(collective_id=0, has_side_effects=True),
    )(
        owner.reshape(1, events),
        item_row,
        out_grad.reshape(events, width),
        bc_proj.reshape(events, 2 * STATE),
        decay_log.reshape(HEADS, events),
        skip_gain,
    )
    got_ids = ids[:, :, :CAP].transpose(1, 0, 2).reshape(1, slots).astype(jnp.int32)

    send = pl.pallas_call(
        pack_kernel,
        name="pack",
        grid=(blocks,),
        out_shape=jax.ShapeDtypeStruct((slots, width), BF16),
        in_specs=[smem, pl.BlockSpec((GROUP * tiles, LANES), lambda i: (i, 0))],
        out_specs=pl.BlockSpec((slots, width), lambda i: (0, 0)),
        scratch_shapes=[pltpu.VMEM((slots * tiles, LANES), F32)],
    )(places, flat)

    got = lax.all_to_all(
        send.reshape(holders, CAP, width), ("tm", "table"), split_axis=0, concat_axis=0, tiled=True
    )

    owned = table.shape[0]
    tall = 256
    tile = pl.BlockSpec((tall, width), lambda i: (i, 0))
    return pl.pallas_call(
        update_kernel,
        name="update",
        grid=(owned // tall,),
        out_shape=(
            jax.ShapeDtypeStruct((owned, width), BF16),
            jax.ShapeDtypeStruct((owned, width), F32),
        ),
        in_specs=[
            pl.BlockSpec((1, slots), lambda i: (0, 0)),
            pl.BlockSpec((slots, width), lambda i: (0, 0)),
            tile,
            tile,
        ],
        out_specs=(tile, tile),
    )(got_ids, got.reshape(slots, width), table, accum)


def solution(mesh):
    placed = (
        P("table", "tm", None),
        P("table", "tm", None),
        P("table", None, "tm"),
        P(),
        P("table", "tm", None),
        P("table", "tm"),
        P(("tm", "table"), None),
        P(("tm", "table"), None),
    )
    return jax.shard_map(
        on_device,
        mesh=mesh,
        in_specs=placed,
        out_specs=(P(("tm", "table"), None), P(("tm", "table"), None)),
        check_vma=False,
    )
```

time: 414 us -> 174 us (0.42)
  other arithmetic: 80.1 us -> 0.01 us
  blocking collectives: 71 us -> 0 us
  local copies, waits for them, and re-layouts: 70.6 us -> 0.8 us
  Pallas kernels: 0 us -> 62.5 us
  waiting for transfers between devices: 128 us -> 96.6 us
  starting transfers between devices: 30.2 us -> 12.7 us
  between operations: 15.2 us -> 0.67 us
  matrix products: 14.5 us -> 0 us
    unnamed x1 -> x0, blocking collectives: 71 us -> none
    pallas_call x0 -> x3, Pallas kernels: none -> 62.5 us  [the longest x1 38.8 us: on_device(): pl.pallas_call(functools.partial(front_kernel, tm_count, table_count), na...]
    all_to_all x4 -> x1, waiting for transfers between devices: 128 us -> 96.6 us  [on_device(): lax.all_to_all(send.reshape(holders, CAP, width), ('tm', 'table'), split_...]
    select_n x33 -> x0, other arithmetic: 31.8 us -> none  [the longest x32 31.8 us: hop(): return jax.tree.map(lambda a, b: jnp.where(reached, a, b), new, before)]
    scatter-add x1 -> x0, other arithmetic: 26.3 us -> none  [on_device(): jax.ops.segment_sum(got_rows.reshape(-1, width).astype(jnp.float32), got_...]
    scatter x2 -> x0, local copies, waits for them, and re-layouts: 20.5 us -> none  [the longest x1 12.3 us: on_device(): jnp.zeros((holders * capacity, width), jnp.bfloat16).at[position]]
    all_to_all x4 -> x1, starting transfers between devices: 30.1 us -> 12.7 us  [on_device(): lax.all_to_all(send.reshape(holders, CAP, width), ('tm', 'table'), split_...]
    dot_general x4 -> x0, matrix products: 14.5 us -> none  [the longest x1 5.27 us: block_rows(): jnp.einsum('hts,thp->shp', mixing, heads_grad, preferred_element_type=jnp...]
  transfers between devices with their start and end apart: 5 -> 1, of which waited for: 3 -> 1; matrix products, arithmetic and copies ran while one was open for 25% -> 0% of each run, Pallas kernels for 0% -> 0%
where the time goes in v2:
time: 174 us; the launch traced here: 173 us
  waiting for transfers between devices  96.6 us (56%)
  Pallas kernels  62.5 us (36%)
  starting transfers between devices  12.7 us (7%)
    all_to_all x1, waiting for transfers between devices, on_device(): lax.all_to_all(send.reshape(holders, CAP, width), ('tm', 'table'), split_...  96.6 us
    pallas_call x1, Pallas kernels, on_device(): pl.pallas_call(functools.partial(front_kernel, tm_count, table_count), na...  38.8 us
    all_to_all x1, starting transfers between devices, on_device(): lax.all_to_all(send.reshape(holders, CAP, width), ('tm', 'table'), split_...  12.7 us
    pallas_call x1, Pallas kernels, on_device(): pl.pallas_call(update_kernel, name='update', grid=(owned // tall,), out_s...  12.1 us
    pallas_call x1, Pallas kernels, on_device(): pl.pallas_call(pack_kernel, name='pack', grid=(blocks,), out_shape=jax.Sh...  11.6 us
  transfers between devices with their start and end apart: 1, of which 1 were waited for; matrix products, arithmetic and copies ran while one was open for 0% of the time, Pallas kernels for 0%

profile of v2, /device:TPU:8, one launch (start us, length us, event | category | flops | bytes accessed | tf_op | source)
XLA Modules:
  0.0 173.2 jit_solution(2740115519305894263)
XLA Ops:
  0.6 38.8 %front.1 = (f32[8192,128]{1,0:T(8,128)}, s32[8,256]{1,0:T(8,128)}, f32[8,32,128]{2,1,0:T(8,128)}) custom-call(s32[1,2048]{1,0:T(1,128)} %bitcast.12, s32[1,2048]{1,0:T(1,128)} %row_ref.1, bf16[2048,512]{1,0:T(8,128)(2,1)} %bitcast.9, bf16[2048,128]{1,0:T(8,128)(2,1)} %bitcast.10, f32[8,2048]{1,0:T(8,128)} %bitcast.11, f32[8]{0:T(128)} %skip_ref.1), custom_call_target="tpu_custom_call" | custom-call | tf_op jit(solution)/shard_map/front/pallas_call | solution.py:363
  39.5 11.6 %pack.1 = bf16[4096,512]{1,0:T(8,128)(2,1)} custom-call(s32[8,256]{1,0:T(8,128)} %get-tuple-element.6.place_ref, f32[8192,128]{1,0:T(8,128)} %get-tuple-element.7.flat_ref), custom_call_target="tpu_custom_call" | custom-call | tf_op jit(solution)/shard_map/pack/pallas_call | solution.py:405
  51.1 0.0 copy-start
  51.1 12.7 %all-to-all-start = ((bf16[256,16,512]{2,1,0:T(8,128)(2,1)}), bf16[256,16,512]{2,1,0:T(8,128)(2,1)}, u32[]{:S(2)}, u32[]{:S(2)}) async-start(bf16[256,16,512]{2,1,0:T(8,128)(2,1)} %bitcast.8), calls=%async_computation | async-start | bytes 8388608 | tf_op jit(solution)/shard_map/all_to_all | solution.py:415
  63.7 0.0 copy-done
  63.8 0.1 copy.11
  63.9 0.7 convert_element_type.9.ids_ref
  64.6 96.6 %all-to-all-done = bf16[256,16,512]{2,1,0:T(8,128)(2,1)} async-done(((bf16[256,16,512]{2,1,0:T(8,128)(2,1)}), bf16[256,16,512]{2,1,0:T(8,128)(2,1)}, u32[]{:S(2)}, u32[]{:S(2)}) %all-to-all-start) | async-done | bytes 4194336 | tf_op jit(solution)/shard_map/all_to_all | solution.py:415
  161.1 12.1 %update.1 = (bf16[1536,512]{1,0:T(8,128)(2,1)}, f32[1536,512]{1,0:T(8,128)}) custom-call(s32[1,4096]{1,0:T(1,128)} %convert_element_type.9.ids_ref, bf16[4096,512]{1,0:T(8,128)(2,1)} %bitcast.6.rows_ref, bf16[1536,512]{1,0:T(8,128)(2,1)} %table_ref.1, f32[1536,512]{1,0:T(8,128)} %accum_ref.1), custom_call_target="tpu_custom_call" | custom-call | tf_op jit(solution)/shard_map/update/pallas_call | solution.py:422
  (1 shorter events, 0.0 us)
Async XLA Ops:
  51.1 12.7 %copy-start = (f32[8,32,128]{2,1,0:T(8,128)S(1)}, f32[8,32,128]{2,1,0:T(8,128)}, u32[]{:S(2)}) copy-start(f32[8,32,128]{2,1,0:T(8,128)} %get-tuple-element.5) | copy-start | bytes 393220
  51.1 110.1 %all-to-all-start = ((bf16[256,16,512]{2,1,0:T(8,128)(2,1)}), bf16[256,16,512]{2,1,0:T(8,128)(2,1)}, u32[]{:S(2)}, u32[]{:S(2)}) async-start(bf16[256,16,512]{2,1,0:T(8,128)(2,1)} %bitcast.8), calls=%async_computation | async-start | bytes 8388608 | tf_op jit(solution)/shard_map/all_to_all | solution.py:415
